TPU v7x, 32 devices: a whole 2x2x4 slice. The times are simulated.
32 devices in a mesh: dom: 8 (over z, y), rhs: 4 (over x, core).
Axes of the slice: x: 2, y: 2, z: 4, core: 2. Of those that a mesh axis runs over, the one named last changes fastest.
Arguments:
- tile_values: float32 [2048, 128, 128], P(('dom', 'rhs')), may hold values from -1 to 3, as said below
- tile_rows: int32 [2048], P(('dom', 'rhs')), may hold values from -1 to 31, as said below
- tile_cols: int32 [2048], P(('dom', 'rhs')), may hold values from 0 to 39, as said below
- send_lists: int32 [8, 2, 4], P('dom'), may hold values from 0 to 31, as said below
- replace_flags: int32 [4], replicated, may hold values from 0 to 1, as said below
- right_side: float32 [4, 256, 128], P(None, ('dom', 'rhs')), may hold values from -25 to 25
- start_iterate: float32 [4, 256, 128], P(None, ('dom', 'rhs')), may hold values from -25 to 25
- start_residual: float32 [4, 256, 128], P(None, ('dom', 'rhs')), may hold values from -25 to 25
- start_direction: float32 [4, 256, 128], P(None, ('dom', 'rhs')), may hold values from -25 to 25
Outputs:
- new_iterate: float32 [4, 256, 128], P(None, ('dom', 'rhs'))
- new_residual: float32 [4, 256, 128], P(None, ('dom', 'rhs'))
- new_direction: float32 [4, 256, 128], P(None, ('dom', 'rhs'))
Inputs may be any that keep to these rules, and one draw needn't show every extreme that they name: `tile_values`: the matrix assembled from all used tile slots is symmetric positive definite. `tile_rows`: -1 marks an empty slot; a used slot of the device with indices (d, r) names a block row from r * 8 to (r + 1) * 8 - 1 of partition d. `tile_cols`: 0 in empty slots. `send_lists`: the 8 entries of one partition are distinct. `replace_flags`: at least one load case is flagged and at least one is not.
All inputs are finite; a program needn't handle non-finite values.
Results may differ from a plain program's by a relative error of at most 0.0003.
Values sent between devices are 32-bit elements; how exact they have to be, the bound alone decides.
A program may use at most 64 MiB of HBM per device.

v0:
```python
import jax
import jax.numpy as jnp
import numpy as np
from jax import lax
from jax.sharding import PartitionSpec as P

SSTEP = 3
highest = lax.Precision.HIGHEST


def with_halo(x, sides, width):
    for axis, dim in sides:
        size, length = (lax.axis_size(axis), x.shape[dim])
        up = [(i, (i + 1) % size) for i in range(size - 1)]
        down = [(j, i) for i, j in up]
        last = lax.slice_in_dim(x, length - width, length, axis=dim)
        first = lax.slice_in_dim(x, 0, width, axis=dim)
        before = lax.ppermute(last, axis, up)
        after = lax.ppermute(first, axis, down)
        x = jnp.concatenate([before, x, after], axis=dim)
    return x


def shift_table(basis_steps):
    basis_width = 2 * basis_steps + 1
    shift_matrix = np.zeros((basis_width, basis_width), np.float32)
    for position in range(basis_steps):
        shift_matrix[position + 1, position] = 1.0
    for position in range(basis_steps - 1):
        shift_matrix[basis_steps + 2 + position, basis_steps + 1 + position] = 1.0
    return shift_matrix


def coefficients(gram_matrix, basis_steps):
    shift_matrix = jnp.asarray(shift_table(basis_steps))
    case_count = gram_matrix.shape[0]
    basis_width = gram_matrix.shape[1]
    eye_matrix = jnp.eye(basis_width, dtype=jnp.float32)
    direction = jnp.broadcast_to(eye_matrix[0], (case_count, basis_width))
    residual = jnp.broadcast_to(eye_matrix[basis_steps + 1], (case_count, basis_width))
    iterate = jnp.zeros((case_count, basis_width), jnp.float32)

    def quadratic(first_vec, second_vec):
        return jnp.einsum("ci,cij,cj->c", first_vec, gram_matrix, second_vec, precision=highest)

    res_norm = quadratic(residual, residual)
    for inner_step in range(basis_steps):
        mapped = jnp.einsum("ij,cj->ci", shift_matrix, direction, precision=highest)
        step_size = res_norm / quadratic(direction, mapped)
        iterate = iterate + step_size[:, None] * direction
        residual = residual - step_size[:, None] * mapped
        next_norm = quadratic(residual, residual)
        direction = residual + (next_norm / res_norm)[:, None] * direction
        res_norm = next_norm
    return (iterate, residual, direction)


def combine(basis_stack, weights):
    return jnp.einsum("icbt,ci->cbt", basis_stack, weights, precision=highest)


def multiply(extended, tile_values, tile_rows, tile_cols, row_start, row_count):
    picked = jnp.take(extended, tile_cols, axis=2)
    product = jnp.einsum("tij,kctj->kcti", tile_values, picked, precision=highest)
    wanted = row_start + lax.iota(jnp.int32, row_count)
    onehot = (tile_rows[:, None] == wanted[None, :]).astype(jnp.float32)
    return jnp.einsum("tb,kcti->kcbi", onehot, product, precision=highest)


def extend(whole_part, own_sends, ghost_width):
    outgoing = jnp.take(whole_part, own_sends, axis=2)
    ghost_rims = with_halo(outgoing, (("dom", 2),), ghost_width)
    return jnp.concatenate(
        [whole_part, ghost_rims[:, :, :ghost_width], ghost_rims[:, :, -ghost_width:]], axis=2
    )


def basis_from(apply_operator, direction, residual, carried):
    direction_powers = [direction]
    residual_powers = [residual]
    carried_image = None
    for power_step in range(SSTEP):
        members = [direction_powers[-1]]
        if power_step < SSTEP - 1:
            members.append(residual_powers[-1])
        if power_step == 0:
            members = members + carried
        mapped = apply_operator(jnp.stack(members))
        direction_powers.append(mapped[0])
        if power_step < SSTEP - 1:
            residual_powers.append(mapped[1])
        if power_step == 0 and carried:
            carried_image = mapped[-1]
    return (jnp.stack(direction_powers + residual_powers), carried_image)


def body(
    tile_values,
    tile_rows,
    tile_cols,
    send_lists,
    replace_flags,
    right_side,
    start_iterate,
    start_residual,
    start_direction,
):
    ghost_width = send_lists.shape[2]
    own_sends = send_lists[0].reshape(2 * ghost_width)
    own_rows = start_residual.shape[1]
    right_part, iterate_part, residual_part, direction_part = (
        right_side,
        start_iterate,
        start_residual,
        start_direction,
    )
    row_start = lax.axis_index("rhs") * own_rows

    def apply_operator(stacked):
        whole_part = lax.all_gather(stacked, "rhs", axis=2, tiled=True)
        return multiply(
            extend(whole_part, own_sends, ghost_width),
            tile_values,
            tile_rows,
            tile_cols,
            row_start,
            own_rows,
        )

    basis_stack, start_image = basis_from(
        apply_operator, direction_part, residual_part, [iterate_part]
    )
    gram_matrix = lax.psum(
        jnp.einsum("icbt,jcbt->cij", basis_stack, basis_stack, precision=highest), ("dom", "rhs")
    )
    iterate_coef, residual_coef, direction_coef = coefficients(gram_matrix, SSTEP)
    new_iterate = iterate_part + combine(basis_stack, iterate_coef)
    recursive = combine(basis_stack, residual_coef)
    new_direction = combine(basis_stack, direction_coef)
    shifted = jnp.einsum(
        "ij,cj->ci", jnp.asarray(shift_table(SSTEP)), iterate_coef, precision=highest
    )
    iterate_image = start_image + combine(basis_stack, shifted)
    replaced = right_part - iterate_image
    new_residual = jnp.where(replace_flags[:, None, None] > 0, replaced, recursive)
    return (new_iterate, new_residual, new_direction)


def solution(mesh):
    placed = (
        P(("dom", "rhs"), None, None),
        P(("dom", "rhs")),
        P(("dom", "rhs")),
        P("dom", None, None),
        P(),
        P(None, ("dom", "rhs"), None),
        P(None, ("dom", "rhs"), None),
        P(None, ("dom", "rhs"), None),
        P(None, ("dom", "rhs"), None),
    )
    return jax.shard_map(
        body,
        mesh=mesh,
        in_specs=placed,
        out_specs=(
            P(None, ("dom", "rhs"), None),
            P(None, ("dom", "rhs"), None),
            P(None, ("dom", "rhs"), None),
        ),
        check_vma=False,
    )
```

profile of v0, /device:TPU:0, one launch (start us, length us, event | category | flops | bytes accessed | tf_op | source)
XLA Modules:
  0.0 127.8 jit_solution(9150678838584309851)
XLA Ops:
  0.6 0.8 reshape_squeeze.6
  1.4 0.8 reshape_squeeze.5
  2.2 0.8 pad_maximum_fusion.2
  2.9 6.8 %all_gather.9 = f32[3,4,32,128]{3,2,1,0:T(8,128)S(1)} all-gather(f32[3,4,8,128]{3,2,1,0:T(8,128)S(1)} %pad_maximum_fusion.2), channel_id=1, replica_groups=mesh['dom'=8,'rhs'=4] {'rhs'}, dimensions={2}, use_global_device_ids=true | all-gather | bytes 245760 | tf_op jit(solution)/shard_map/all_gather | solution.py:120
  9.8 0.1 copy.18
  9.9 0.6 gather_fusion
  10.5 0.1 fusion.31
  10.6 3.6 %collective-permute-start = (f32[3,4,4,128]{3,2,1,0:T(4,128)S(1)}, f32[3,4,4,128]{3,2,1,0:T(4,128)S(1)}, u32[]{:S(2)}, u32[]{:S(2)}) collective-permute-start(f32[3,4,4,128]{3,2,1,0:T(4,128)S(1)} %get-tuple-element.3), channel_id=1, source_target_pairs={{0,4},{4,8},{8,12},{12,16},{16,20},{20,24},{24,28},{1,5},{5,9},{9,... | collective-permute-start | bytes 73736 | tf_op jit(solution)/shard_map/ppermute | solution.py:18
  14.3 1.3 %collective-permute-start.1 = (f32[3,4,4,128]{3,2,1,0:T(4,128)S(1)}, f32[3,4,4,128]{3,2,1,0:T(4,128)S(1)}, u32[]{:S(2)}, u32[]{:S(2)}) collective-permute-start(f32[3,4,4,128]{3,2,1,0:T(4,128)S(1)} %get-tuple-element.4), channel_id=1, source_target_pairs={{4,0},{8,4},{12,8},{16,12},{20,16},{24,20},{28,24},{5,1},{9,5},{13... | collective-permute-start | bytes 73736 | tf_op jit(solution)/shard_map/ppermute | solution.py:19
  15.6 0.7 compare_select_fusion.2
  16.2 0.7 compare_and_fusion.1
  16.9 0.7 constant_dynamic-update-slice_fusion.2
  17.6 2.3 %collective-permute-done.1 = f32[3,4,4,128]{3,2,1,0:T(4,128)S(1)} collective-permute-done((f32[3,4,4,128]{3,2,1,0:T(4,128)S(1)}, f32[3,4,4,128]{3,2,1,0:T(4,128)S(1)}, u32[]{:S(2)}, u32[]{:S(2)}) %collective-permute-start.1) | collective-permute-done | bytes 24608 | tf_op jit(solution)/shard_map/ppermute | solution.py:19
  20.1 0.8 gather_fusion.1
  20.9 8.7 %fusion.2 = f32[64,3,4,128]{3,2,1,0:T(4,128)S(1)} fusion(f32[64,128,128]{2,1,0:T(8,128)} %param.11, f32[64,3,4,128]{3,2,1,0:T(4,128)S(1)} %gather_fusion.1, pred[64]{0:T(512)(128)(4,1)S(1)} %compare_and_fusion.1), kind=kOutput, calls=%fused_computation.8 | convolution fusion | flops 151093248 | bytes 4980800 | tf_op jit(solution)/shard_map/tij,kctj->kcti/dot_general | solution.py:64
  29.6 0.3 convolution_bitcast_fusion.1
  29.9 5.4 %all_gather.10 = f32[2,4,32,128]{3,2,1,0:T(8,128)S(1)} all-gather(f32[2,4,8,128]{3,2,1,0:T(8,128)S(1)} %stack.26), channel_id=1, replica_groups=mesh['dom'=8,'rhs'=4] {'rhs'}, dimensions={2}, use_global_device_ids=true | all-gather | bytes 163840 | tf_op jit(solution)/shard_map/all_gather | solution.py:120
  35.3 0.1 copy.21
  35.4 0.6 gather_fusion.2
  36.0 0.1 fusion.32
  36.1 4.3 %collective-permute-start.2 = (f32[2,4,4,128]{3,2,1,0:T(4,128)S(1)}, f32[2,4,4,128]{3,2,1,0:T(4,128)S(1)}, u32[]{:S(2)}, u32[]{:S(2)}) collective-permute-start(f32[2,4,4,128]{3,2,1,0:T(4,128)S(1)} %get-tuple-element.7), channel_id=1, source_target_pairs={{0,4},{4,8},{8,12},{12,16},{16,20},{20,24},{24,28},{1,5},{5,9},{9,... | collective-permute-start | bytes 49160 | tf_op jit(solution)/shard_map/ppermute | solution.py:18
  40.4 1.3 %collective-permute-start.3 = (f32[2,4,4,128]{3,2,1,0:T(4,128)S(1)}, f32[2,4,4,128]{3,2,1,0:T(4,128)S(1)}, u32[]{:S(2)}, u32[]{:S(2)}) collective-permute-start(f32[2,4,4,128]{3,2,1,0:T(4,128)S(1)} %get-tuple-element.8), channel_id=1, source_target_pairs={{4,0},{8,4},{12,8},{16,12},{20,16},{24,20},{28,24},{5,1},{9,5},{13... | collective-permute-start | bytes 49160 | tf_op jit(solution)/shard_map/ppermute | solution.py:19
  41.7 0.1 collective-permute-done.2
  41.8 4.2 %collective-permute-done.3 = f32[2,4,4,128]{3,2,1,0:T(4,128)S(1)} collective-permute-done((f32[2,4,4,128]{3,2,1,0:T(4,128)S(1)}, f32[2,4,4,128]{3,2,1,0:T(4,128)S(1)}, u32[]{:S(2)}, u32[]{:S(2)}) %collective-permute-start.3) | collective-permute-done | bytes 16416 | tf_op jit(solution)/shard_map/ppermute | solution.py:19
  46.1 0.7 gather_fusion.3
  46.9 8.4 %fusion = f32[64,2,4,128]{3,2,1,0:T(4,128)S(1)} fusion(f32[64,128,128]{2,1,0:T(8,128)} %param.11, f32[64,2,4,128]{3,2,1,0:T(4,128)S(1)} %gather_fusion.3, pred[64]{0:T(512)(128)(4,1)S(1)} %compare_and_fusion.1), kind=kOutput, calls=%fused_computation.6 | convolution fusion | flops 100728832 | bytes 4718656 | tf_op jit(solution)/shard_map/tij,kctj->kcti/dot_general | solution.py:64
  55.3 0.2 convolution_bitcast_fusion.2
  55.5 5.2 %all_gather.11 = f32[1,4,32,128]{3,2,1,0:T(8,128)S(1)} all-gather(f32[1,4,8,128]{3,2,1,0:T(8,128)S(1)} %get-tuple-element.5), channel_id=1, replica_groups=mesh['dom'=8,'rhs'=4] {'rhs'}, dimensions={2}, use_global_device_ids=true | all-gather | bytes 81920 | tf_op jit(solution)/shard_map/all_gather | solution.py:120
  60.8 0.6 gather_fusion.4
  61.4 0.1 bitcast_select_fusion
  61.5 3.4 %collective-permute-start.4 = (f32[1,4,4,128]{3,2,1,0:T(4,128)S(1)}, f32[1,4,4,128]{3,2,1,0:T(4,128)S(1)}, u32[]{:S(2)}, u32[]{:S(2)}) collective-permute-start(f32[1,4,4,128]{3,2,1,0:T(4,128)S(1)} %get-tuple-element.9), channel_id=1, source_target_pairs={{0,4},{4,8},{8,12},{12,16},{16,20},{20,24},{24,28},{1,5},{5,9},{9,... | collective-permute-start | bytes 24584 | tf_op jit(solution)/shard_map/ppermute | solution.py:18
  64.9 1.3 %collective-permute-start.5 = (f32[1,4,4,128]{3,2,1,0:T(4,128)S(1)}, f32[1,4,4,128]{3,2,1,0:T(4,128)S(1)}, u32[]{:S(2)}, u32[]{:S(2)}) collective-permute-start(f32[1,4,4,128]{3,2,1,0:T(4,128)S(1)} %get-tuple-element.10), channel_id=1, source_target_pairs={{4,0},{8,4},{12,8},{16,12},{20,16},{24,20},{28,24},{5,1},{9,5},{13... | collective-permute-start | bytes 24584 | tf_op jit(solution)/shard_map/ppermute | solution.py:19
  66.3 4.2 %collective-permute-done.5 = f32[1,4,4,128]{3,2,1,0:T(4,128)S(1)} collective-permute-done((f32[1,4,4,128]{3,2,1,0:T(4,128)S(1)}, f32[1,4,4,128]{3,2,1,0:T(4,128)S(1)}, u32[]{:S(2)}, u32[]{:S(2)}) %collective-permute-start.5) | collective-permute-done | bytes 8224 | tf_op jit(solution)/shard_map/ppermute | solution.py:19
  70.5 0.7 gather_fusion.5
  71.2 8.4 %convolution_bitcast_fusion = f32[4,64,128]{2,0,1:T(4,128)S(1)} fusion(f32[64,128,128]{2,1,0:T(8,128)} %param.11, f32[64,4,128]{2,1,0:T(4,128)S(1)} %gather_fusion.5, pred[64]{0:T(512)(128)(4,1)S(1)} %compare_and_fusion.1), kind=kOutput, calls=%fused_computation.10 | convolution fusion | flops 50364416 | bytes 4456512 | tf_op jit(solution)/shard_map/tij,kctj->kcti/dot_general | solution.py:64
  79.5 0.2 fusion.4
  79.8 0.4 convolution_bitcast_fusion.3
  80.2 41.2 %psum.7 = f32[4,7,7]{2,1,0:T(8,128)S(1)} all-reduce(f32[4,7,7]{2,1,0:T(8,128)S(1)} %convolution_bitcast_fusion.3), channel_id=1, replica_groups=mesh['dom'=8,'rhs'=4] {'dom','rhs'}, use_global_device_ids=true, to_apply=%region_0.1 | all-reduce | flops 196 | bytes 1568 | tf_op jit(solution)/shard_map/psum | solution.py:133
  121.4 0.2 fusion.53
  121.6 0.1 multiply_reduce_fusion.6
  121.7 0.2 fusion.54
  121.9 0.2 multiply_reduce_fusion.5
  122.2 0.1 multiply_subtract_fusion.2
  122.2 0.2 fusion.55
  122.4 0.2 multiply_reduce_fusion.4
  122.6 0.1 multiply_add_fusion.3
  122.7 0.2 fusion.56
  122.8 0.2 multiply_reduce_fusion.3
  123.1 0.1 multiply_subtract_fusion.1
  123.2 0.2 fusion.57
  123.3 0.1 multiply_reduce_fusion.2
  123.5 0.1 multiply_add_fusion.2
  123.6 0.2 fusion.58
  123.7 0.2 multiply_reduce_fusion.1
  124.1 0.2 fusion.60
  124.2 0.1 multiply_reduce_fusion
  124.4 0.1 multiply_add_fusion
  124.4 0.9 fusion.15
  125.4 0.1 fusion.59
  125.5 0.3 fusion.19
  125.8 0.3 fusion.17
  126.2 0.3 fusion.21
  126.5 0.6 add.82
  127.1 0.7 fusion.35
  (47 shorter events, 0.5 us)
Async XLA Ops:
  0.6 29.0 %copy-start.4 = (s32[64]{0:T(128)S(1)}, s32[64]{0:T(128)}, u32[]{:S(2)}) copy-start(s32[64]{0:T(128)} %param.12) | copy-start | bytes 772
  10.6 7.0 %collective-permute-start = (f32[3,4,4,128]{3,2,1,0:T(4,128)S(1)}, f32[3,4,4,128]{3,2,1,0:T(4,128)S(1)}, u32[]{:S(2)}, u32[]{:S(2)}) collective-permute-start(f32[3,4,4,128]{3,2,1,0:T(4,128)S(1)} %get-tuple-element.3), channel_id=1, source_target_pairs={{0,4},{4,8},{8,12},{12,16},{16,20},{20,24},{24,28},{1,5},{5,9},{9,... | collective-permute-start | bytes 73736 | tf_op jit(solution)/shard_map/ppermute | solution.py:18
  14.3 5.7 %collective-permute-start.1 = (f32[3,4,4,128]{3,2,1,0:T(4,128)S(1)}, f32[3,4,4,128]{3,2,1,0:T(4,128)S(1)}, u32[]{:S(2)}, u32[]{:S(2)}) collective-permute-start(f32[3,4,4,128]{3,2,1,0:T(4,128)S(1)} %get-tuple-element.4), channel_id=1, source_target_pairs={{4,0},{8,4},{12,8},{16,12},{20,16},{24,20},{28,24},{5,1},{9,5},{13... | collective-permute-start | bytes 73736 | tf_op jit(solution)/shard_map/ppermute | solution.py:19
  29.6 36.6 %copy-start.5 = (s32[4]{0:T(128)S(1)}, s32[4]{0:T(128)}, u32[]{:S(2)}) copy-start(s32[4]{0:T(128)} %param.15) | copy-start | bytes 52
  36.1 5.8 %collective-permute-start.2 = (f32[2,4,4,128]{3,2,1,0:T(4,128)S(1)}, f32[2,4,4,128]{3,2,1,0:T(4,128)S(1)}, u32[]{:S(2)}, u32[]{:S(2)}) collective-permute-start(f32[2,4,4,128]{3,2,1,0:T(4,128)S(1)} %get-tuple-element.7), channel_id=1, source_target_pairs={{0,4},{4,8},{8,12},{12,16},{16,20},{20,24},{24,28},{1,5},{5,9},{9,... | collective-permute-start | bytes 49160 | tf_op jit(solution)/shard_map/ppermute | solution.py:18
  40.4 5.6 %collective-permute-start.3 = (f32[2,4,4,128]{3,2,1,0:T(4,128)S(1)}, f32[2,4,4,128]{3,2,1,0:T(4,128)S(1)}, u32[]{:S(2)}, u32[]{:S(2)}) collective-permute-start(f32[2,4,4,128]{3,2,1,0:T(4,128)S(1)} %get-tuple-element.8), channel_id=1, source_target_pairs={{4,0},{8,4},{12,8},{16,12},{20,16},{24,20},{28,24},{5,1},{9,5},{13... | collective-permute-start | bytes 49160 | tf_op jit(solution)/shard_map/ppermute | solution.py:19
  46.9 32.9 %copy-start.2 = (f32[4,8,128]{2,1,0:T(8,128)S(1)}, f32[4,8,128]{2,1,0:T(8,128)}, u32[]{:S(2)}) copy-start(f32[4,8,128]{2,1,0:T(8,128)} %param.18) | copy-start | bytes 49156
  55.3 66.6 %copy-start.1 = (f32[7,7]{1,0:T(8,128)S(1)}, f32[7,7]{1,0:T(8,128)}, u32[]{:S(2)}) copy-start(f32[7,7]{1,0:T(8,128)} %constant.87.clone) | copy-start | bytes 592
  55.3 71.2 %copy-start = (f32[4,8,128]{2,1,0:T(8,128)S(1)}, f32[4,8,128]{2,1,0:T(8,128)}, u32[]{:S(2)}) copy-start(f32[4,8,128]{2,1,0:T(8,128)} %param.17) | copy-start | bytes 49156
  55.3 71.8 %copy-start.3 = (f32[4,8,128]{2,1,0:T(8,128)S(1)}, f32[4,8,128]{2,1,0:T(8,128)}, u32[]{:S(2)}) copy-start(f32[4,8,128]{2,1,0:T(8,128)} %param.16) | copy-start | bytes 49156
  61.5 4.8 %collective-permute-start.4 = (f32[1,4,4,128]{3,2,1,0:T(4,128)S(1)}, f32[1,4,4,128]{3,2,1,0:T(4,128)S(1)}, u32[]{:S(2)}, u32[]{:S(2)}) collective-permute-start(f32[1,4,4,128]{3,2,1,0:T(4,128)S(1)} %get-tuple-element.9), channel_id=1, source_target_pairs={{0,4},{4,8},{8,12},{12,16},{16,20},{20,24},{24,28},{1,5},{5,9},{9,... | collective-permute-start | bytes 24584 | tf_op jit(solution)/shard_map/ppermute | solution.py:18
  64.9 5.5 %collective-permute-start.5 = (f32[1,4,4,128]{3,2,1,0:T(4,128)S(1)}, f32[1,4,4,128]{3,2,1,0:T(4,128)S(1)}, u32[]{:S(2)}, u32[]{:S(2)}) collective-permute-start(f32[1,4,4,128]{3,2,1,0:T(4,128)S(1)} %get-tuple-element.10), channel_id=1, source_target_pairs={{4,0},{8,4},{12,8},{16,12},{20,16},{24,20},{28,24},{5,1},{9,5},{13... | collective-permute-start | bytes 24584 | tf_op jit(solution)/shard_map/ppermute | solution.py:19
where the time goes:
time: 128 us
  blocking collectives  58.7 us (46%)
  matrix products  30.5 us (24%)
  starting transfers between devices  15.2 us (12%)
  waiting for transfers between devices  10.9 us (9%)
  local copies, waits for them, and re-layouts  6.71 us (5%)
  other arithmetic  4.71 us (4%)
    psum x1, blocking collectives, body(): lax.psum(jnp.einsum('icbt,jcbt->cij', basis_stack, basis_stack, precision...  41.2 us
    dot_general x3, matrix products, multiply(): jnp.einsum('tij,kctj->kcti', tile_values, picked, precision=highest)  25.5 us
    all_gather x3, blocking collectives, apply_operator(): whole_part = lax.all_gather(stacked, 'rhs', axis=2, tiled=True)  17.5 us
    ppermute x3, starting transfers between devices, with_halo(): before = lax.ppermute(last, axis, up)  11.4 us
    ppermute x3, waiting for transfers between devices, with_halo(): after = lax.ppermute(first, axis, down)  10.7 us
    ppermute x3, starting transfers between devices, with_halo(): after = lax.ppermute(first, axis, down)  3.88 us
  transfers between devices with their start and end apart: 6, of which 4 were waited for; matrix products, arithmetic and copies ran while one was open for 2% of the time, Pallas kernels for 0%

commit v1 on v0

--- a/solution.py
+++ b/solution.py
@@ -131,7 +131,8 @@
         apply_operator, direction_part, residual_part, [iterate_part]
     )
     gram_matrix = lax.psum(
-        jnp.einsum("icbt,jcbt->cij", basis_stack, basis_stack, precision=highest), ("dom", "rhs")
+        lax.psum(jnp.einsum("icbt,jcbt->cij", basis_stack, basis_stack, precision=highest), "rhs"),
+        "dom",
     )
     iterate_coef, residual_coef, direction_coef = coefficients(gram_matrix, SSTEP)
     new_iterate = iterate_part + combine(basis_stack, iterate_coef)

time: 128 us -> 133 us (1.039)
  blocking collectives: 58.7 us -> 62.9 us
    psum x0 -> x1, blocking collectives: none -> 35.3 us  [body(): lax.psum(lax.psum(jnp.einsum('icbt,jcbt->cij', basis_stack, basis_stack,...]
    psum x1, blocking collectives: 41.2 us -> 10.1 us  [body(): lax.psum(jnp.einsum('icbt,jcbt->cij', basis_stack, basis_stack, precision...]
where the time goes in v1:
time: 133 us; the launch traced here: 132 us
  blocking collectives  62.9 us (47%)
  matrix products  30.5 us (23%)
  starting transfers between devices  15.2 us (11%)
  waiting for transfers between devices  10.9 us (8%)
  local copies, waits for them, and re-layouts  6.71 us (5%)
  other arithmetic  4.7 us (4%)
    psum x1, blocking collectives, body(): lax.psum(lax.psum(jnp.einsum('icbt,jcbt->cij', basis_stack, basis_stack,...  35.3 us
    dot_general x3, matrix products, multiply(): jnp.einsum('tij,kctj->kcti', tile_values, picked, precision=highest)  25.5 us
    all_gather x3, blocking collectives, apply_operator(): whole_part = lax.all_gather(stacked, 'rhs', axis=2, tiled=True)  17.5 us
    ppermute x3, starting transfers between devices, with_halo(): before = lax.ppermute(last, axis, up)  11.4 us
    ppermute x3, waiting for transfers between devices, with_halo(): after = lax.ppermute(first, axis, down)  10.7 us
    psum x1, blocking collectives, body(): lax.psum(jnp.einsum('icbt,jcbt->cij', basis_stack, basis_stack, precision...  10.1 us
    ppermute x3, starting transfers between devices, with_halo(): after = lax.ppermute(first, axis, down)  3.88 us
  transfers between devices with their start and end apart: 6, of which 4 were waited for; matrix products, arithmetic and copies ran while one was open for 2% of the time, Pallas kernels for 0%

profile of v1, /device:TPU:0, one launch (start us, length us, event | category | flops | bytes accessed | tf_op | source)
XLA Modules:
  0.0 131.9 jit_solution(12613601301889497057)
XLA Ops:
  0.6 0.8 reshape_squeeze.6
  1.4 0.8 reshape_squeeze.5
  2.2 0.8 pad_maximum_fusion.2
  2.9 6.8 %all_gather.9 = f32[3,4,32,128]{3,2,1,0:T(8,128)S(1)} all-gather(f32[3,4,8,128]{3,2,1,0:T(8,128)S(1)} %pad_maximum_fusion.2), channel_id=1, replica_groups=mesh['dom'=8,'rhs'=4] {'rhs'}, dimensions={2}, use_global_device_ids=true | all-gather | bytes 245760 | tf_op jit(solution)/shard_map/all_gather | solution.py:120
  9.8 0.1 copy.18
  9.9 0.6 gather_fusion
  10.5 0.1 fusion.31
  10.6 3.6 %collective-permute-start = (f32[3,4,4,128]{3,2,1,0:T(4,128)S(1)}, f32[3,4,4,128]{3,2,1,0:T(4,128)S(1)}, u32[]{:S(2)}, u32[]{:S(2)}) collective-permute-start(f32[3,4,4,128]{3,2,1,0:T(4,128)S(1)} %get-tuple-element.3), channel_id=1, source_target_pairs={{0,4},{4,8},{8,12},{12,16},{16,20},{20,24},{24,28},{1,5},{5,9},{9,... | collective-permute-start | bytes 73736 | tf_op jit(solution)/shard_map/ppermute | solution.py:18
  14.3 1.3 collective-permute-start.1
  15.6 0.7 compare_select_fusion.2
  16.2 0.7 compare_and_fusion.1
  16.9 0.7 constant_dynamic-update-slice_fusion.2
  17.6 2.3 %collective-permute-done.1 = f32[3,4,4,128]{3,2,1,0:T(4,128)S(1)} collective-permute-done((f32[3,4,4,128]{3,2,1,0:T(4,128)S(1)}, f32[3,4,4,128]{3,2,1,0:T(4,128)S(1)}, u32[]{:S(2)}, u32[]{:S(2)}) %collective-permute-start.1) | collective-permute-done | bytes 24608 | tf_op jit(solution)/shard_map/ppermute | solution.py:19
  20.1 0.8 gather_fusion.1
  20.9 8.7 %fusion.2 = f32[64,3,4,128]{3,2,1,0:T(4,128)S(1)} fusion(f32[64,128,128]{2,1,0:T(8,128)} %param.11, f32[64,3,4,128]{3,2,1,0:T(4,128)S(1)} %gather_fusion.1, pred[64]{0:T(512)(128)(4,1)S(1)} %compare_and_fusion.1), kind=kOutput, calls=%fused_computation.8 | convolution fusion | flops 151093248 | bytes 4980800 | tf_op jit(solution)/shard_map/tij,kctj->kcti/dot_general | solution.py:64
  29.6 0.3 convolution_bitcast_fusion.1
  29.9 5.4 %all_gather.10 = f32[2,4,32,128]{3,2,1,0:T(8,128)S(1)} all-gather(f32[2,4,8,128]{3,2,1,0:T(8,128)S(1)} %stack.26), channel_id=1, replica_groups=mesh['dom'=8,'rhs'=4] {'rhs'}, dimensions={2}, use_global_device_ids=true | all-gather | bytes 163840 | tf_op jit(solution)/shard_map/all_gather | solution.py:120
  35.3 0.1 copy.21
  35.4 0.6 gather_fusion.2
  36.0 0.1 fusion.32
  36.1 4.3 %collective-permute-start.2 = (f32[2,4,4,128]{3,2,1,0:T(4,128)S(1)}, f32[2,4,4,128]{3,2,1,0:T(4,128)S(1)}, u32[]{:S(2)}, u32[]{:S(2)}) collective-permute-start(f32[2,4,4,128]{3,2,1,0:T(4,128)S(1)} %get-tuple-element.7), channel_id=1, source_target_pairs={{0,4},{4,8},{8,12},{12,16},{16,20},{20,24},{24,28},{1,5},{5,9},{9,... | collective-permute-start | bytes 49160 | tf_op jit(solution)/shard_map/ppermute | solution.py:18
  40.4 1.3 collective-permute-start.3
  41.7 0.1 collective-permute-done.2
  41.8 4.2 %collective-permute-done.3 = f32[2,4,4,128]{3,2,1,0:T(4,128)S(1)} collective-permute-done((f32[2,4,4,128]{3,2,1,0:T(4,128)S(1)}, f32[2,4,4,128]{3,2,1,0:T(4,128)S(1)}, u32[]{:S(2)}, u32[]{:S(2)}) %collective-permute-start.3) | collective-permute-done | bytes 16416 | tf_op jit(solution)/shard_map/ppermute | solution.py:19
  46.1 0.7 gather_fusion.3
  46.9 8.4 %fusion = f32[64,2,4,128]{3,2,1,0:T(4,128)S(1)} fusion(f32[64,128,128]{2,1,0:T(8,128)} %param.11, f32[64,2,4,128]{3,2,1,0:T(4,128)S(1)} %gather_fusion.3, pred[64]{0:T(512)(128)(4,1)S(1)} %compare_and_fusion.1), kind=kOutput, calls=%fused_computation.6 | convolution fusion | flops 100728832 | bytes 4718656 | tf_op jit(solution)/shard_map/tij,kctj->kcti/dot_general | solution.py:64
  55.3 0.2 convolution_bitcast_fusion.2
  55.5 5.2 %all_gather.11 = f32[1,4,32,128]{3,2,1,0:T(8,128)S(1)} all-gather(f32[1,4,8,128]{3,2,1,0:T(8,128)S(1)} %get-tuple-element.5), channel_id=1, replica_groups=mesh['dom'=8,'rhs'=4] {'rhs'}, dimensions={2}, use_global_device_ids=true | all-gather | bytes 81920 | tf_op jit(solution)/shard_map/all_gather | solution.py:120
  60.8 0.6 gather_fusion.4
  61.4 0.1 bitcast_select_fusion
  61.5 3.4 %collective-permute-start.4 = (f32[1,4,4,128]{3,2,1,0:T(4,128)S(1)}, f32[1,4,4,128]{3,2,1,0:T(4,128)S(1)}, u32[]{:S(2)}, u32[]{:S(2)}) collective-permute-start(f32[1,4,4,128]{3,2,1,0:T(4,128)S(1)} %get-tuple-element.9), channel_id=1, source_target_pairs={{0,4},{4,8},{8,12},{12,16},{16,20},{20,24},{24,28},{1,5},{5,9},{9,... | collective-permute-start | bytes 24584 | tf_op jit(solution)/shard_map/ppermute | solution.py:18
  64.9 1.3 collective-permute-start.5
  66.3 4.2 %collective-permute-done.5 = f32[1,4,4,128]{3,2,1,0:T(4,128)S(1)} collective-permute-done((f32[1,4,4,128]{3,2,1,0:T(4,128)S(1)}, f32[1,4,4,128]{3,2,1,0:T(4,128)S(1)}, u32[]{:S(2)}, u32[]{:S(2)}) %collective-permute-start.5) | collective-permute-done | bytes 8224 | tf_op jit(solution)/shard_map/ppermute | solution.py:19
  70.5 0.7 gather_fusion.5
  71.2 8.4 %convolution_bitcast_fusion = f32[4,64,128]{2,0,1:T(4,128)S(1)} fusion(f32[64,128,128]{2,1,0:T(8,128)} %param.11, f32[64,4,128]{2,1,0:T(4,128)S(1)} %gather_fusion.5, pred[64]{0:T(512)(128)(4,1)S(1)} %compare_and_fusion.1), kind=kOutput, calls=%fused_computation.10 | convolution fusion | flops 50364416 | bytes 4456512 | tf_op jit(solution)/shard_map/tij,kctj->kcti/dot_general | solution.py:64
  79.5 0.2 fusion.4
  79.8 0.4 convolution_bitcast_fusion.3
  80.2 10.1 %psum.14 = f32[4,7,7]{2,1,0:T(8,128)S(1)} all-reduce(f32[4,7,7]{2,1,0:T(8,128)S(1)} %convolution_bitcast_fusion.3), channel_id=1, replica_groups=mesh['dom'=8,'rhs'=4] {'rhs'}, use_global_device_ids=true, to_apply=%region_0.1 | all-reduce | flops 196 | bytes 1568 | tf_op jit(solution)/shard_map/psum | solution.py:134
  90.3 35.3 %psum.15 = f32[4,7,7]{2,1,0:T(8,128)S(1)} all-reduce(f32[4,7,7]{2,1,0:T(8,128)S(1)} %psum.14), channel_id=1, replica_groups=mesh['dom'=8,'rhs'=4] {'dom'}, use_global_device_ids=true, to_apply=%region_1.2 | all-reduce | flops 196 | bytes 1568 | tf_op jit(solution)/shard_map/psum | solution.py:133
  125.6 0.2 fusion.53
  125.8 0.1 multiply_reduce_fusion.6
  125.9 0.2 fusion.54
  126.0 0.2 multiply_reduce_fusion.5
  126.4 0.2 fusion.55
  126.6 0.2 multiply_reduce_fusion.4
  126.8 0.1 multiply_add_fusion.3
  126.8 0.2 fusion.56
  127.0 0.2 multiply_reduce_fusion.3
  127.3 0.1 multiply_subtract_fusion.1
  127.3 0.2 fusion.57
  127.5 0.1 multiply_reduce_fusion.2
  127.6 0.1 multiply_add_fusion.2
  127.7 0.2 fusion.58
  127.9 0.2 multiply_reduce_fusion.1
  128.2 0.2 fusion.60
  128.4 0.1 multiply_reduce_fusion
  128.5 0.1 multiply_add_fusion
  128.6 0.9 fusion.15
  129.5 0.1 fusion.59
  129.7 0.3 fusion.19
  130.0 0.3 fusion.17
  130.3 0.3 fusion.21
  130.6 0.6 add.84
  131.3 0.7 fusion.35
  (48 shorter events, 0.6 us)
Async XLA Ops:
  0.6 29.0 %copy-start.4 = (s32[64]{0:T(128)S(1)}, s32[64]{0:T(128)}, u32[]{:S(2)}) copy-start(s32[64]{0:T(128)} %param.12) | copy-start | bytes 772
  10.6 7.0 %collective-permute-start = (f32[3,4,4,128]{3,2,1,0:T(4,128)S(1)}, f32[3,4,4,128]{3,2,1,0:T(4,128)S(1)}, u32[]{:S(2)}, u32[]{:S(2)}) collective-permute-start(f32[3,4,4,128]{3,2,1,0:T(4,128)S(1)} %get-tuple-element.3), channel_id=1, source_target_pairs={{0,4},{4,8},{8,12},{12,16},{16,20},{20,24},{24,28},{1,5},{5,9},{9,... | collective-permute-start | bytes 73736 | tf_op jit(solution)/shard_map/ppermute | solution.py:18
  14.3 5.7 %collective-permute-start.1 = (f32[3,4,4,128]{3,2,1,0:T(4,128)S(1)}, f32[3,4,4,128]{3,2,1,0:T(4,128)S(1)}, u32[]{:S(2)}, u32[]{:S(2)}) collective-permute-start(f32[3,4,4,128]{3,2,1,0:T(4,128)S(1)} %get-tuple-element.4), channel_id=1, source_target_pairs={{4,0},{8,4},{12,8},{16,12},{20,16},{24,20},{28,24},{5,1},{9,5},{13... | collective-permute-start | bytes 73736 | tf_op jit(solution)/shard_map/ppermute | solution.py:19
  29.6 36.6 %copy-start.5 = (s32[4]{0:T(128)S(1)}, s32[4]{0:T(128)}, u32[]{:S(2)}) copy-start(s32[4]{0:T(128)} %param.15) | copy-start | bytes 52
  36.1 5.8 %collective-permute-start.2 = (f32[2,4,4,128]{3,2,1,0:T(4,128)S(1)}, f32[2,4,4,128]{3,2,1,0:T(4,128)S(1)}, u32[]{:S(2)}, u32[]{:S(2)}) collective-permute-start(f32[2,4,4,128]{3,2,1,0:T(4,128)S(1)} %get-tuple-element.7), channel_id=1, source_target_pairs={{0,4},{4,8},{8,12},{12,16},{16,20},{20,24},{24,28},{1,5},{5,9},{9,... | collective-permute-start | bytes 49160 | tf_op jit(solution)/shard_map/ppermute | solution.py:18
  40.4 5.6 %collective-permute-start.3 = (f32[2,4,4,128]{3,2,1,0:T(4,128)S(1)}, f32[2,4,4,128]{3,2,1,0:T(4,128)S(1)}, u32[]{:S(2)}, u32[]{:S(2)}) collective-permute-start(f32[2,4,4,128]{3,2,1,0:T(4,128)S(1)} %get-tuple-element.8), channel_id=1, source_target_pairs={{4,0},{8,4},{12,8},{16,12},{20,16},{24,20},{28,24},{5,1},{9,5},{13... | collective-permute-start | bytes 49160 | tf_op jit(solution)/shard_map/ppermute | solution.py:19
  46.9 32.9 %copy-start.2 = (f32[4,8,128]{2,1,0:T(8,128)S(1)}, f32[4,8,128]{2,1,0:T(8,128)}, u32[]{:S(2)}) copy-start(f32[4,8,128]{2,1,0:T(8,128)} %param.18) | copy-start | bytes 49156
  55.3 70.8 %copy-start.1 = (f32[7,7]{1,0:T(8,128)S(1)}, f32[7,7]{1,0:T(8,128)}, u32[]{:S(2)}) copy-start(f32[7,7]{1,0:T(8,128)} %constant.87.clone) | copy-start | bytes 592
  55.3 75.3 %copy-start = (f32[4,8,128]{2,1,0:T(8,128)S(1)}, f32[4,8,128]{2,1,0:T(8,128)}, u32[]{:S(2)}) copy-start(f32[4,8,128]{2,1,0:T(8,128)} %param.17) | copy-start | bytes 49156
  55.3 75.9 %copy-start.3 = (f32[4,8,128]{2,1,0:T(8,128)S(1)}, f32[4,8,128]{2,1,0:T(8,128)}, u32[]{:S(2)}) copy-start(f32[4,8,128]{2,1,0:T(8,128)} %param.16) | copy-start | bytes 49156
  61.5 4.8 %collective-permute-start.4 = (f32[1,4,4,128]{3,2,1,0:T(4,128)S(1)}, f32[1,4,4,128]{3,2,1,0:T(4,128)S(1)}, u32[]{:S(2)}, u32[]{:S(2)}) collective-permute-start(f32[1,4,4,128]{3,2,1,0:T(4,128)S(1)} %get-tuple-element.9), channel_id=1, source_target_pairs={{0,4},{4,8},{8,12},{12,16},{16,20},{20,24},{24,28},{1,5},{5,9},{9,... | collective-permute-start | bytes 24584 | tf_op jit(solution)/shard_map/ppermute | solution.py:18
  64.9 5.5 %collective-permute-start.5 = (f32[1,4,4,128]{3,2,1,0:T(4,128)S(1)}, f32[1,4,4,128]{3,2,1,0:T(4,128)S(1)}, u32[]{:S(2)}, u32[]{:S(2)}) collective-permute-start(f32[1,4,4,128]{3,2,1,0:T(4,128)S(1)} %get-tuple-element.10), channel_id=1, source_target_pairs={{4,0},{8,4},{12,8},{16,12},{20,16},{24,20},{28,24},{5,1},{9,5},{13... | collective-permute-start | bytes 24584 | tf_op jit(solution)/shard_map/ppermute | solution.py:19
